TPU v7x, 32 devices: a whole 2x2x4 slice. The times are simulated.
32 devices in a mesh: dp: 2 (over x), ts: 16 (over z, y, core).
Axes of the slice: x: 2, y: 2, z: 4, core: 2. Of those that a mesh axis runs over, the one named last changes fastest.
Arguments:
- clip_video: bfloat16 [64, 4, 40, 128], P(('dp', 'ts')), may hold values from -6 to 6
- conv_weight: bfloat16 [3, 3, 3, 128, 128], replicated, may hold values from -0.109375 to 0.109375
- embed_weight: bfloat16 [128, 5120], replicated, may hold values from -0.5 to 0.5
- gain_spatial: float32 [5120], replicated, may hold values from 0.5 to 1.5
- gain_temporal: float32 [5120], replicated, may hold values from 0.5 to 1.5
- input_spatial: bfloat16 [5120, 384], P(('dp', 'ts')), may hold values from -0.078125 to 0.078125
- input_temporal: bfloat16 [5120, 384], P(('dp', 'ts')), may hold values from -0.078125 to 0.078125
- output_spatial: bfloat16 [128, 5120], replicated, may hold values from -2 to 2
- output_temporal: bfloat16 [128, 5120], replicated, may hold values from -2 to 2
- cotangent: bfloat16 [64, 4, 40, 5120], P(('dp', 'ts')), may hold values from -6 to 6
Outputs:
- layer_output: bfloat16 [64, 4, 40, 5120], P(('dp', 'ts'))
- grad_spatial: float32 [5120, 384], P(('dp', 'ts'))
All inputs are finite; a program needn't handle non-finite values.
Results may differ from a plain program's by a relative error of at most 0.015.
Values may be sent and summed in bfloat16 or wider, within the bound.
A program may use at most 128 MiB of HBM per device.

v0:
```python
import jax
import jax.numpy as jnp
from jax import lax
from jax.sharding import PartitionSpec as P

FR = 16
epsilon = 1e-06
masked = -1e30
F32 = jnp.float32
BF16 = jnp.bfloat16


def mm(a, b, dims=((1,), (0,))):
    return lax.dot_general(a, b, (dims, ((), ())), preferred_element_type=F32)


def mm_t(a, b):
    return mm(a, b, ((1,), (1,)))


def t_mm(a, b):
    return mm(a, b, ((0,), (0,)))


def wide_mm(a, b):
    high = b.astype(BF16)
    low = (b - high.astype(F32)).astype(BF16)
    return mm(a, high) + mm(a, low)


def conv_local(volume, weight, count):
    frames, height, columns, channels = volume.shape
    padded = jnp.pad(volume, ((0, 0), (1, 1), (1, 1), (0, 0)))
    summed = jnp.zeros((count * height * columns, weight.shape[-1]), F32)
    for a in range(3):
        for b in range(3):
            for e in range(3):
                window = padded[2 - a : 2 - a + count, b : b + height, e : e + columns, :]
                summed = summed + mm(window.reshape(-1, channels), weight[a, b, e])
    return summed


def attend_forward(q, k, v, allowed):
    scores = mm_t(q, k) * q.shape[-1] ** (-0.5)
    scores = jnp.where(allowed, scores, masked)
    raised = jnp.exp(scores - jnp.max(scores, axis=-1, keepdims=True))
    attend = raised / jnp.sum(raised, axis=-1, keepdims=True)
    return (mm(attend.astype(BF16), v).astype(BF16), attend)


def attend_backward(q, k, v, attend, g):
    scale = q.shape[-1] ** (-0.5)
    grad_attend = mm_t(g, v)
    grad_values = t_mm(attend.astype(BF16), g)
    inner = jnp.sum(grad_attend * attend, axis=-1, keepdims=True)
    grad_scores = (attend * (grad_attend - inner)).astype(BF16)
    grad_q = mm(grad_scores, k) * scale
    grad_k = t_mm(grad_scores, q) * scale
    return jnp.concatenate([grad_q, grad_k, grad_values], axis=-1).astype(BF16)


def shards(
    clip_video,
    conv_weight,
    embed_weight,
    gain_spatial,
    gain_temporal,
    input_spatial,
    input_temporal,
    output_spatial,
    output_temporal,
    cotangent,
):
    frames, height, columns, channels = clip_video.shape
    rows, triple = input_spatial.shape
    head = triple // 3
    width = embed_weight.shape[-1]
    places = height * columns
    tokens = frames * places
    ts = lax.axis_size("ts")
    team = FR // frames
    share = places // team
    groups = [[c * team + i for i in range(team)] for c in range(ts // team)]
    me = lax.axis_index("dp") * ts + lax.axis_index("ts")
    route = [(i - 1, i) for i in range(1, ts)]
    prior = lax.ppermute(clip_video, "ts", route)
    volume = jnp.concatenate([prior, clip_video], axis=0)
    basis = jnp.concatenate([embed_weight, output_spatial], axis=0)
    window = lax.dynamic_slice(basis, (0, me * rows), (basis.shape[0], rows)).astype(F32)
    gain_s = lax.dynamic_slice(gain_spatial, (me * rows,), (rows,))
    gain_t = lax.dynamic_slice(gain_temporal, (me * rows,), (rows,))
    embed_rows = (window[:channels] * gain_s).astype(BF16)
    part = jnp.concatenate(
        [mm(embed_rows, input_spatial), mm((window * gain_t).astype(BF16), input_temporal)], axis=0
    )
    mixed = lax.psum(part.astype(BF16), ("dp", "ts"))
    map_space, map_time = (mixed[:channels], mixed[channels:])
    gram = mm_t(basis, basis)
    cotangent_rows = cotangent.reshape(tokens, width)
    grad_mix_time = mm_t(cotangent_rows, output_temporal).astype(BF16)
    grad_direct = mm_t(cotangent_rows, output_spatial)
    features = jax.nn.gelu(conv_local(volume, conv_weight, frames), approximate=True).astype(BF16)
    squares = jnp.sum(
        wide_mm(features, gram[:channels, :channels]) * features.astype(F32), axis=-1, keepdims=True
    )
    factor_one = lax.rsqrt(jnp.maximum(squares, 0.0) / width + epsilon)
    packed_one = (mm(features, map_space) * factor_one).astype(BF16)
    place = jnp.arange(tokens)
    same_frame = place[:, None] // places == place[None, :] // places
    q, k, v = (packed_one[:, :head], packed_one[:, head : 2 * head], packed_one[:, 2 * head :])
    mixture_one, attend_one = attend_forward(q, k, v, same_frame)
    joint = jnp.concatenate([features, mixture_one], axis=-1)
    spread = wide_mm(joint, gram)
    squares = jnp.sum(spread * joint.astype(F32), axis=-1, keepdims=True)
    factor_two = lax.rsqrt(jnp.maximum(squares, 0.0) / width + epsilon)
    packed_two = (mm(joint, map_time) * factor_two).astype(BF16)
    sent = jnp.concatenate([packed_two, grad_mix_time], axis=-1).reshape(frames, places, 4 * head)
    got = lax.all_to_all(
        sent, "ts", split_axis=1, concat_axis=0, tiled=True, axis_index_groups=groups
    ).reshape(FR * share, 4 * head)
    spot = jnp.arange(FR * share)
    allowed = (spot[:, None] % share == spot[None, :] % share) & (spot[:, None] >= spot[None, :])
    tq, tk, tv, tg = (got[:, i * head : (i + 1) * head] for i in range(4))
    mixture_two, attend_two = attend_forward(tq, tk, tv, allowed)
    grad_two = attend_backward(tq, tk, tv, attend_two, tg)
    back = jnp.concatenate([mixture_two, grad_two], axis=-1).reshape(FR, share, 4 * head)
    home = lax.all_to_all(
        back, "ts", split_axis=0, concat_axis=1, tiled=True, axis_index_groups=groups
    ).reshape(tokens, 4 * head)
    mixture_two, grad_two = (home[:, :head], home[:, head:])
    output = mm(
        jnp.concatenate([joint, mixture_two], axis=-1),
        jnp.concatenate([basis, output_temporal], axis=0),
    ).astype(BF16)
    inner = jnp.sum(grad_two.astype(F32) * packed_two.astype(F32), axis=-1, keepdims=True)
    grad_mix_one = (
        grad_direct
        + factor_two * mm_t(grad_two, map_time[channels:])
        - factor_two**2 * inner / width * spread[:, channels:]
    ).astype(BF16)
    grad_one = attend_backward(q, k, v, attend_one, grad_mix_one)
    scaled = (features.astype(F32) * factor_one).astype(BF16)
    core = lax.psum(t_mm(scaled, grad_one).astype(BF16), ("dp", "ts"))
    return (output.reshape(frames, height, columns, width), t_mm(embed_rows, core))


def solution(mesh):
    placed = (
        P(("dp", "ts"), None, None, None),
        P(),
        P(),
        P(),
        P(),
        P(("dp", "ts"), None),
        P(("dp", "ts"), None),
        P(),
        P(),
        P(("dp", "ts"), None, None, None),
    )
    return jax.shard_map(
        shards,
        mesh=mesh,
        in_specs=placed,
        out_specs=(P(("dp", "ts"), None, None, None), P(("dp", "ts"), None)),
        check_vma=False,
    )
```

profile of v0, /device:TPU:8, one launch (start us, length us, event | category | flops | bytes accessed | tf_op | source)
XLA Modules:
  0.0 330.4 jit_solution(1640951019662262618)
XLA Ops:
  7.2 2.2 collective-permute-start
  9.4 2.5 constant_dynamic-update-slice_fusion.3
  11.9 2.5 constant_dynamic-update-slice_fusion.2
  14.4 1.0 dynamic-slice_convert_fusion
  15.4 0.8 dynamic_slice.10
  16.3 0.8 dynamic_slice.11
  17.0 1.2 convolution_convert_fusion.1
  18.2 1.1 convolution_convert_fusion.3
  20.1 3.5 %fusion.148 = f32[256,256]{1,0:T(8,128)S(1)} fusion(bf16[256,5120]{1,0:T(8,128)(2,1)} %constant_dynamic-update-slice_fusion.2), kind=kOutput, calls=%fused_computation.247 | convolution fusion | flops 671088640 | bytes 2883584 | tf_op jit(solution)/shard_map/dot_general | solution.py:14
  23.7 1.0 convolution_convert_fusion.4
  25.1 0.8 copy-done.8
  30.7 120.0 %all-reduce.4.cloned.1.call-done = bf16[384,384]{1,0:T(8,128)(2,1)} async-done(((bf16[384,384]{1,0:T(8,128)(2,1)}), bf16[384,384]{1,0:T(8,128)(2,1)}) %all-reduce.4.cloned.1.call-update) | async-done | bytes 294928 | tf_op jit(solution)/shard_map/psum | solution.py:96
  150.8 1.1 fusion.7
  153.5 0.9 multiply_reduce_fusion.3
  155.4 1.0 copy.12
  156.5 4.2 %all-to-all-start = ((bf16[2,160,512]{2,0,1:T(2,128)(2,1)}), bf16[2,160,512]{2,0,1:T(2,128)(2,1)}, u32[]{:S(2)}, u32[]{:S(2)}) async-start(bf16[2,160,512]{2,0,1:T(2,128)(2,1)} %copy.12), calls=%async_computation | async-start | bytes 655360 | tf_op jit(solution)/shard_map/all_to_all | solution.py:118
  160.7 6.2 %all-to-all-done = bf16[2,160,512]{2,0,1:T(2,128)(2,1)} async-done(((bf16[2,160,512]{2,0,1:T(2,128)(2,1)}), bf16[2,160,512]{2,0,1:T(2,128)(2,1)}, u32[]{:S(2)}, u32[]{:S(2)}) %all-to-all-start) | async-done | bytes 327712 | tf_op jit(solution)/shard_map/all_to_all | solution.py:118
  166.9 1.8 copy.13
  168.7 1.8 reshape.248
  170.5 1.2 fusion.147
  171.8 1.2 convolution_convert_fusion.7
  174.9 1.8 reshape.249
  176.7 10.8 %all_to_all.30 = bf16[16,20,512]{2,1,0:T(8,128)(2,1)S(1)} all-to-all(bf16[16,20,512]{2,1,0:T(8,128)(2,1)} %reshape.249), channel_id=1, replica_groups={{0,1,2,3,4,5,6,7},{8,9,10,11,12,13,14,15},{16,17,18,19,20,21,22,23},{24..., dimensions={0} | all-to-all | bytes 655360 | tf_op jit(solution)/shard_map/all_to_all | solution.py:127
  187.8 0.9 copy.15
  188.7 1.8 reshape.250
  190.5 1.2 multiply_reduce_fusion.1
  191.7 1.3 convolution_multiply_fusion.6
  193.0 2.4 fusion.16
  196.6 1.0 convolution_convert_fusion.2
  197.7 5.7 %convolution_convert_fusion = bf16[320,5120]{1,0:T(8,128)(2,1)} fusion(bf16[128,5120]{1,0:T(8,128)(2,1)} %param.18, bf16[128,5120]{1,0:T(8,128)(2,1)} %param.17, bf16[128,5120]{1,0:T(8,128)(2,1)} %param.12, bf16[320,128]{1,0:T(8,128)(2,1)S(1)} %slice-done, bf16[320,128]{1,0:T(8,128)(2,1)S(1)} %convolution_convert_fusion.8, bf16[320,128]{1,0:T(8,128)(2,1)S(1)} %fusion.43), kind=kOutput, calls=%fused_computation | convolution fusion | flops 1272463360 | bytes 7454720 | tf_op jit(solution)/shard_map/dot_general | solution.py:14
  203.3 118.4 %all-reduce.6.cloned.1.call-done = bf16[128,384]{1,0:T(8,128)(2,1)} async-done(((bf16[128,384]{1,0:T(8,128)(2,1)}), bf16[128,384]{1,0:T(8,128)(2,1)}) %all-reduce.6.cloned.1.call-update) | async-done | bytes 98320 | tf_op jit(solution)/shard_map/psum | solution.py:143
  321.7 1.9 fusion.129
  (94 shorter events, 11.9 us)
Async XLA Ops:
  7.2 16.5 %copy-start = (bf16[2,4,40,5120]{3,2,1,0:T(8,128)(2,1)S(1)}, bf16[2,4,40,5120]{3,2,1,0:T(8,128)(2,1)}, u32[]{:S(2)}) copy-start(bf16[2,4,40,5120]{3,2,1,0:T(8,128)(2,1)} %param.19) | copy-start | bytes 9830404
  7.2 143.6 %all-reduce.4.cloned.1.call-start = ((), (), s32[]{:S(2)}) async-start(), calls=%async_computation.2 | async-start | bytes 589824 | tf_op jit(solution)/shard_map/psum | solution.py:96
  7.2 17.5 %collective-permute-start = (bf16[2,4,40,128]{3,2,1,0:T(8,128)(2,1)}, bf16[2,4,40,128]{3,2,1,0:T(8,128)(2,1)S(1)}, u32[]{:S(2)}, u32[]{:S(2)}) collective-permute-start(bf16[2,4,40,128]{3,2,1,0:T(8,128)(2,1)} %param.10), channel_id=1, source_target_pairs={{0,1},{1,2},{2,3},{3,4},{4,5},{5,6},{6,7},{7,8},{8,9},{9,10},{10,1... | collective-permute-start | bytes 245768 | tf_op jit(solution)/shard_map/ppermute | solution.py:86
  9.4 7.6 %copy-start.13 = (bf16[160,384]{1,0:T(8,128)(2,1)S(1)}, bf16[160,384]{1,0:T(8,128)(2,1)}, u32[]{:S(2)}) copy-start(bf16[160,384]{1,0:T(8,128)(2,1)} %param.16) | copy-start | bytes 368644
  15.4 2.8 copy-start.6
  20.1 3.6 %copy-start.5 = (bf16[128,5120]{1,0:T(8,128)(2,1)S(1)}, bf16[128,5120]{1,0:T(8,128)(2,1)}, u32[]{:S(2)}) copy-start(bf16[128,5120]{1,0:T(8,128)(2,1)} %param.18) | copy-start | bytes 3932164
  23.6 6.8 %copy-start.3 = (f32[256,256]{1,0:T(8,128)}, f32[256,256]{1,0:T(8,128)S(1)}, u32[]{:S(2)}) copy-start(f32[256,256]{1,0:T(8,128)S(1)} %fusion.148) | copy-start | bytes 786436
  23.7 1.1 copy-start.12
  24.7 1.2 copy-start.8
  150.7 2.5 copy-start.4
  151.9 1.3 copy-start.10
  151.9 2.5 copy-start.14
  152.2 0.8 copy-start.1
  154.7 0.7 copy-start.7
  156.5 10.4 %all-to-all-start = ((bf16[2,160,512]{2,0,1:T(2,128)(2,1)}), bf16[2,160,512]{2,0,1:T(2,128)(2,1)}, u32[]{:S(2)}, u32[]{:S(2)}) async-start(bf16[2,160,512]{2,0,1:T(2,128)(2,1)} %copy.12), calls=%async_computation | async-start | bytes 655360 | tf_op jit(solution)/shard_map/all_to_all | solution.py:118
  160.7 161.0 %all-reduce.6.cloned.1.call-start = ((), (), s32[]{:S(2)}) async-start(), calls=%async_computation.3 | async-start | bytes 196608 | tf_op jit(solution)/shard_map/psum | solution.py:143
  170.5 2.5 copy-start.9
  193.0 2.4 copy-start.2
  193.0 2.4 copy-start.11
  195.7 1.9 slice-start
Sparse Core Ops, SparseCore 0:
  20.2 130.4 all-reduce.3
  197.8 123.8 all-reduce.5
where the time goes:
time: 331 us; the launch traced here: 330 us
  waiting for transfers between devices  245 us (74%)
  matrix products  31.3 us (9%)
  local copies, waits for them, and re-layouts  18.4 us (6%)
  between operations  14.5 us (4%)
  blocking collectives  10.8 us (3%)
  starting transfers between devices  6.42 us (2%)
  other arithmetic  4.29 us (1%)
    psum x1, waiting for transfers between devices, shards(): mixed = lax.psum(part.astype(BF16), ('dp', 'ts'))  120 us
    psum x1, waiting for transfers between devices, shards(): core = lax.psum(t_mm(scaled, grad_one).astype(BF16), ('dp', 'ts'))  118 us
    dot_general x54, matrix products, mm(): return lax.dot_general(a, b, (dims, ((), ())), preferred_element_type=F32)  31.3 us
    all_to_all x1, blocking collectives, shards(): lax.all_to_all(back, 'ts', split_axis=0, concat_axis=1, tiled=True, axis_...  10.8 us
  transfers between devices with their start and end apart: 4, of which 3 were waited for; matrix products, arithmetic and copies ran while one was open for 8% of the time, Pallas kernels for 0%

commit v1 on v0

--- a/solution.py
+++ b/solution.py
@@ -140,7 +140,9 @@
     ).astype(BF16)
     grad_one = attend_backward(q, k, v, attend_one, grad_mix_one)
     scaled = (features.astype(F32) * factor_one).astype(BF16)
-    core = lax.psum(t_mm(scaled, grad_one).astype(BF16), ("dp", "ts"))
+    x = t_mm(scaled, grad_one).astype(BF16)
+    pieces = lax.all_gather(x, ("dp", "ts"))
+    core = jnp.sum(pieces, axis=0)
     return (output.reshape(frames, height, columns, width), t_mm(embed_rows, core))
 
 

time: 331 us -> 271 us (0.82); the launches traced: 330 us -> 267 us
  waiting for transfers between devices: 245 us -> 178 us
    psum x1 -> x0, waiting for transfers between devices: 118 us -> none  [shards(): core = lax.psum(t_mm(scaled, grad_one).astype(BF16), ('dp', 'ts'))]
    all_gather x0 -> x1, waiting for transfers between devices: none -> 51.9 us  [shards(): pieces = lax.all_gather(x, ('dp', 'ts'))]
  transfers between devices with their start and end apart: 4 -> 4, of which waited for: 3 -> 3; matrix products, arithmetic and copies ran while one was open for 8% -> 10% of each run, Pallas kernels for 0% -> 0%
where the time goes in v1:
time: 271 us; the launch traced here: 267 us
  waiting for transfers between devices  178 us (66%)
  matrix products  31.2 us (12%)
  local copies, waits for them, and re-layouts  18.5 us (7%)
  between operations  14.5 us (5%)
  blocking collectives  10.8 us (4%)
  other arithmetic  7.26 us (3%)
  starting transfers between devices  6.41 us (2%)
    psum x1, waiting for transfers between devices, shards(): mixed = lax.psum(part.astype(BF16), ('dp', 'ts'))  120 us
    all_gather x1, waiting for transfers between devices, shards(): pieces = lax.all_gather(x, ('dp', 'ts'))  51.9 us
    dot_general x54, matrix products, mm(): return lax.dot_general(a, b, (dims, ((), ())), preferred_element_type=F32)  31.2 us
    all_to_all x1, blocking collectives, shards(): lax.all_to_all(back, 'ts', split_axis=0, concat_axis=1, tiled=True, axis_...  10.8 us
    all_to_all x1, waiting for transfers between devices, shards(): lax.all_to_all(sent, 'ts', split_axis=1, concat_axis=0, tiled=True, axis_...  6.24 us
  transfers between devices with their start and end apart: 4, of which 3 were waited for; matrix products, arithmetic and copies ran while one was open for 10% of the time, Pallas kernels for 0%

profile of v1, /device:TPU:8, one launch (start us, length us, event | category | flops | bytes accessed | tf_op | source)
XLA Modules:
  0.0 266.9 jit_solution(2848588338631703226)
XLA Ops:
  7.2 2.2 collective-permute-start
  9.4 2.5 constant_dynamic-update-slice_fusion.3
  11.9 2.5 constant_dynamic-update-slice_fusion.2
  14.4 1.0 dynamic-slice_convert_fusion
  15.4 0.8 dynamic_slice.10
  17.0 1.2 convolution_convert_fusion.1
  18.2 1.1 convolution_convert_fusion.3
  20.1 3.5 %fusion.148 = f32[256,256]{1,0:T(8,128)S(1)} fusion(bf16[256,5120]{1,0:T(8,128)(2,1)} %constant_dynamic-update-slice_fusion.2), kind=kOutput, calls=%fused_computation.247 | convolution fusion | flops 671088640 | bytes 2883584 | tf_op jit(solution)/shard_map/dot_general | solution.py:14
  23.6 1.0 convolution_convert_fusion.4
  25.1 0.8 copy-done.9
  30.7 120.1 %all-reduce.3.cloned.1.call-done = bf16[384,384]{1,0:T(8,128)(2,1)} async-done(((bf16[384,384]{1,0:T(8,128)(2,1)}), bf16[384,384]{1,0:T(8,128)(2,1)}) %all-reduce.3.cloned.1.call-update) | async-done | bytes 294928 | tf_op jit(solution)/shard_map/psum | solution.py:96
  150.8 1.1 fusion.7
  153.5 0.9 multiply_reduce_fusion.3
  155.4 1.1 copy.12
  156.5 4.2 %all-to-all-start = ((bf16[2,160,512]{2,0,1:T(2,128)(2,1)}), bf16[2,160,512]{2,0,1:T(2,128)(2,1)}, u32[]{:S(2)}, u32[]{:S(2)}) async-start(bf16[2,160,512]{2,0,1:T(2,128)(2,1)} %copy.12), calls=%async_computation | async-start | bytes 655360 | tf_op jit(solution)/shard_map/all_to_all | solution.py:118
  160.7 6.2 %all-to-all-done = bf16[2,160,512]{2,0,1:T(2,128)(2,1)} async-done(((bf16[2,160,512]{2,0,1:T(2,128)(2,1)}), bf16[2,160,512]{2,0,1:T(2,128)(2,1)}, u32[]{:S(2)}, u32[]{:S(2)}) %all-to-all-start) | async-done | bytes 327712 | tf_op jit(solution)/shard_map/all_to_all | solution.py:118
  166.9 1.8 copy.13
  168.7 1.8 reshape.248
  170.5 1.2 fusion.147
  171.8 1.2 convolution_convert_fusion.7
  174.9 1.8 reshape.249
  176.7 10.8 %all_to_all.30 = bf16[16,20,512]{2,1,0:T(8,128)(2,1)S(1)} all-to-all(bf16[16,20,512]{2,1,0:T(8,128)(2,1)} %reshape.249), channel_id=1, replica_groups={{0,1,2,3,4,5,6,7},{8,9,10,11,12,13,14,15},{16,17,18,19,20,21,22,23},{24..., dimensions={0} | all-to-all | bytes 655360 | tf_op jit(solution)/shard_map/all_to_all | solution.py:127
  187.8 0.9 copy.15
  188.8 1.8 reshape.250
  190.6 1.2 multiply_reduce_fusion.1
  191.8 1.3 convolution_multiply_fusion.6
  193.1 2.4 fusion.16
  196.7 1.0 convolution_convert_fusion.2
  197.7 5.7 %convolution_convert_fusion = bf16[320,5120]{1,0:T(8,128)(2,1)} fusion(bf16[128,5120]{1,0:T(8,128)(2,1)} %param.18, bf16[128,5120]{1,0:T(8,128)(2,1)} %param.17, bf16[128,5120]{1,0:T(8,128)(2,1)} %param.12, bf16[320,128]{1,0:T(8,128)(2,1)S(1)} %slice-done, bf16[320,128]{1,0:T(8,128)(2,1)S(1)} %convolution_convert_fusion.8, bf16[320,128]{1,0:T(8,128)(2,1)S(1)} %fusion.43), kind=kOutput, calls=%fused_computation | convolution fusion | flops 1272463360 | bytes 7454720 | tf_op jit(solution)/shard_map/dot_general | solution.py:14
  203.4 51.9 %all-gather.3.cloned.1.call-done = bf16[4096,384]{1,0:T(8,128)(2,1)} async-done(((bf16[128,384]{1,0:T(8,128)(2,1)}), bf16[4096,384]{1,0:T(8,128)(2,1)}) %all-gather.3.cloned.1.call-update) | async-done | bytes 3145744 | tf_op jit(solution)/shard_map/all_gather | solution.py:144
  255.3 3.0 %reduce_sum.82 = bf16[128,384]{1,0:T(8,128)(2,1)} reduce(bf16[32,128,384]{2,1,0:T(8,128)(2,1)} %bitcast.166, bf16[]{:T(256)} %constant.28.clone.1), dimensions={0}, to_apply=%region_10.11 | reduce | flops 1523712 | bytes 3244034 | tf_op jit(solution)/shard_map/reduce_sum | solution.py:145
  258.3 1.8 fusion.129
  (97 shorter events, 12.7 us)
Async XLA Ops:
  7.2 16.4 %copy-start = (bf16[2,4,40,5120]{3,2,1,0:T(8,128)(2,1)S(1)}, bf16[2,4,40,5120]{3,2,1,0:T(8,128)(2,1)}, u32[]{:S(2)}) copy-start(bf16[2,4,40,5120]{3,2,1,0:T(8,128)(2,1)} %param.19) | copy-start | bytes 9830404
  7.2 143.6 %all-reduce.3.cloned.1.call-start = ((), (), s32[]{:S(2)}) async-start(), calls=%async_computation.2 | async-start | bytes 589824 | tf_op jit(solution)/shard_map/psum | solution.py:96
  7.2 17.5 %collective-permute-start = (bf16[2,4,40,128]{3,2,1,0:T(8,128)(2,1)}, bf16[2,4,40,128]{3,2,1,0:T(8,128)(2,1)S(1)}, u32[]{:S(2)}, u32[]{:S(2)}) collective-permute-start(bf16[2,4,40,128]{3,2,1,0:T(8,128)(2,1)} %param.10), channel_id=1, source_target_pairs={{0,1},{1,2},{2,3},{3,4},{4,5},{5,6},{6,7},{7,8},{8,9},{9,10},{10,1... | collective-permute-start | bytes 245768 | tf_op jit(solution)/shard_map/ppermute | solution.py:86
  9.4 7.6 %copy-start.14 = (bf16[160,384]{1,0:T(8,128)(2,1)S(1)}, bf16[160,384]{1,0:T(8,128)(2,1)}, u32[]{:S(2)}) copy-start(bf16[160,384]{1,0:T(8,128)(2,1)} %param.16) | copy-start | bytes 368644
  15.4 2.8 %copy-start.6 = (f32[256,160]{1,0:T(8,128)}, f32[256,160]{1,0:T(8,128)S(1)}, u32[]{:S(2)}) copy-start(f32[256,160]{1,0:T(8,128)S(1)} %dynamic-slice_convert_fusion) | copy-start | bytes 491524
  20.1 3.6 %copy-start.5 = (bf16[128,5120]{1,0:T(8,128)(2,1)S(1)}, bf16[128,5120]{1,0:T(8,128)(2,1)}, u32[]{:S(2)}) copy-start(bf16[128,5120]{1,0:T(8,128)(2,1)} %param.18) | copy-start | bytes 3932164
  23.6 6.8 %copy-start.3 = (f32[256,256]{1,0:T(8,128)}, f32[256,256]{1,0:T(8,128)S(1)}, u32[]{:S(2)}) copy-start(f32[256,256]{1,0:T(8,128)S(1)} %fusion.148) | copy-start | bytes 786436
  23.6 1.1 copy-start.13
  24.7 1.2 copy-start.9
  150.8 2.5 copy-start.4
  151.9 1.3 copy-start.11
  151.9 2.5 copy-start.15
  152.2 0.8 copy-start.1
  154.7 0.7 copy-start.8
  156.5 10.4 %all-to-all-start = ((bf16[2,160,512]{2,0,1:T(2,128)(2,1)}), bf16[2,160,512]{2,0,1:T(2,128)(2,1)}, u32[]{:S(2)}, u32[]{:S(2)}) async-start(bf16[2,160,512]{2,0,1:T(2,128)(2,1)} %copy.12), calls=%async_computation | async-start | bytes 655360 | tf_op jit(solution)/shard_map/all_to_all | solution.py:118
  160.7 94.6 %all-gather.3.cloned.1.call-start = ((), (), s32[]{:S(2)}) async-start(), calls=%async_computation.3 | async-start | bytes 3244032 | tf_op jit(solution)/shard_map/all_gather | solution.py:144
  170.5 2.5 copy-start.10
  193.1 2.4 copy-start.2
  193.1 2.4 copy-start.12
  195.8 1.9 slice-start
  203.4 54.9 %copy-start.7 = (f32[256,160]{1,0:T(8,128)S(1)}, f32[256,160]{1,0:T(8,128)}, u32[]{:S(2)}) copy-start(f32[256,160]{1,0:T(8,128)} %copy-done.6) | copy-start | bytes 491524
Sparse Core Ops, SparseCore 0:
  20.2 130.5 all-reduce.2
  197.8 57.4 all-gather.2
